TPU v7x, 32 devices: a whole 2x2x4 slice. The times are simulated.
32 devices in a mesh: grp: 2 (over x), wide: 16 (over z, y, core).
Axes of the slice: x: 2, y: 2, z: 4, core: 2. Of those that a mesh axis runs over, the one named last changes fastest.
Arguments:
- queries: bfloat16 [256, 4096], P(('grp', 'wide')), parts along dimension 0, may hold values from -8 to 8
- draft_keys: bfloat16 [256, 512], P(('grp', 'wide')), parts along dimension 0, may hold values from -8 to 8
- draft_values: bfloat16 [256, 512], P(('grp', 'wide')), parts along dimension 0, may hold values from -24 to 24
- cache_keys: bfloat16 [262144, 128], P(('grp', 'wide')), parts along dimension 0, may hold values from -8 to 8
- cache_values: bfloat16 [262144, 128], P(('grp', 'wide')), parts along dimension 0, may hold values from -24 to 24
- block_owner: int32 [32], P('grp'), parts along dimension 0, may hold values from 0 to 15, each once
- block_lengths: int32 [32], P('grp'), parts along dimension 0, may hold values from 1024 to 8192, as said below
- draft_mask: int32 [4, 64, 64], P('grp'), parts along dimension 0, may hold values from 0 to 1, as said below
- out_weight: bfloat16 [4096, 8192], P(None, 'wide'), may hold values from -1 to 1
- norm_gain: float32 [8192], replicated, may hold values from 0.25 to 1.75
- gate_weight: bfloat16 [8192, 14336], P(None, 'wide'), may hold values from -0.0625 to 0.0625
- up_weight: bfloat16 [8192, 14336], P(None, 'wide'), may hold values from -0.0625 to 0.0625
Outputs:
- projected: bfloat16 [256, 8192], P('grp', 'wide'), parts along dimension 0
- hidden: bfloat16 [256, 14336], P('grp', 'wide'), parts along dimension 0
There are 2 independent parts, one for each index of `grp`. A program takes and returns all parts, laid end to end along the dimension named above; an argument that names none is the same for every part. Nothing has to cross between parts.
Inputs may be any that keep to these rules, and one draw needn't show every extreme that they name: `block_owner`: each device holds exactly one block. `block_lengths`: at most 8192 rows a block, and some block has exactly 8192 rows. In each sequence row 0 is the root of a tree in which every other row's parent lies 1 to 4 rows before it; draft_mask[s, i, t] is 1 exactly when t is i or an ancestor of i.
All inputs are finite; a program needn't handle non-finite values.
Results may differ from a plain program's by a relative error of at most 0.02.
Values may be sent and summed in bfloat16 or wider, within the bound.
A program may use at most 128 MiB of HBM per device.

v0:
```python
import math
import jax
import jax.numpy as jnp
from jax import lax
from jax.sharding import PartitionSpec as P

very_low = -1e30
epsilon = 1e-05


def block_update(state, query_rows, block_keys, block_values, valid, scale):
    running, total, weighted = state
    scores = (
        jnp.einsum("igc,kc->igk", query_rows, block_keys, preferred_element_type=jnp.float32)
        * scale
    )
    scores = jnp.where(valid, scores, very_low)
    newest = jnp.maximum(running, jnp.max(scores, axis=-1))
    factor = jnp.exp(running - newest)
    weights = jnp.where(valid, jnp.exp(scores - newest[..., None]), 0.0)
    total = total * factor + jnp.sum(weights, axis=-1)
    weighted = weighted * factor[..., None] + jnp.einsum(
        "igk,kc->igc",
        weights.astype(jnp.bfloat16),
        block_values,
        preferred_element_type=jnp.float32,
    )
    return (newest, total, weighted)


def attend(query_rows, keys, values, length, own_keys, own_values, own_valid):
    block_size = min(512, keys.shape[0])
    scale = 1.0 / math.sqrt(query_rows.shape[2])
    rows_count = query_rows.shape[0]
    heads = query_rows.shape[1]
    state = (
        jnp.full((rows_count, heads), very_low, jnp.float32),
        jnp.zeros((rows_count, heads), jnp.float32),
        jnp.zeros((rows_count, heads, query_rows.shape[2]), jnp.float32),
    )
    offsets = jnp.arange(block_size, dtype=jnp.int32)

    def advance(number, carry):
        begin = (number * block_size).astype(jnp.int32)
        block_keys = lax.dynamic_slice_in_dim(keys, begin, block_size, 0)
        block_values = lax.dynamic_slice_in_dim(values, begin, block_size, 0)
        valid = (begin + offsets < length)[None, None, :]
        return block_update(carry, query_rows, block_keys, block_values, valid, scale)

    count = (length + block_size - 1) // block_size
    state = lax.fori_loop(jnp.int32(0), count, advance, state)
    return block_update(state, query_rows, own_keys, own_values, own_valid[:, None, :], scale)


def per_device(
    queries,
    draft_keys,
    draft_values,
    cache_keys,
    cache_values,
    block_owner,
    block_lengths,
    draft_mask,
    out_weight,
    norm_gain,
    gate_weight,
    up_weight,
):
    devices = lax.axis_size("wide")
    own_index = lax.axis_index("wide")
    head_size = cache_keys.shape[1]
    key_heads = draft_keys.shape[1] // head_size
    group_width = queries.shape[1] // key_heads
    group = group_width // head_size
    sequences = draft_mask.shape[0]
    draft_rows = draft_mask.shape[1]
    all_rows = sequences * draft_rows
    local_rows = queries.shape[0]
    heads_all = key_heads * group
    blocks_per_pair = devices // (sequences * key_heads)
    device_ids = jnp.arange(devices, dtype=jnp.int32)
    owned = (block_owner[None, :] == device_ids[:, None]).astype(jnp.int32)
    device_block = jnp.sum(owned * device_ids[None, :], axis=1)
    device_pair = device_block // blocks_per_pair
    device_sequence = device_pair // key_heads
    device_head = device_pair % key_heads
    device_length = jnp.sum(owned * block_lengths[None, :], axis=1)
    picker = (device_ids == own_index).astype(jnp.int32)
    own_block = jnp.sum(picker * device_block)
    own_sequence = jnp.sum(picker * device_sequence)
    own_head = jnp.sum(picker * device_head)
    own_length = jnp.sum(picker * device_length)
    is_last = own_block % blocks_per_pair == blocks_per_pair - 1
    row_start = own_sequence * draft_rows
    head_numbers = jnp.arange(key_heads, dtype=jnp.int32)
    every_query, every_key, every_value = (
        lax.all_gather(queries, "wide", axis=0, tiled=True),
        lax.all_gather(draft_keys, "wide", axis=0, tiled=True),
        lax.all_gather(draft_values, "wide", axis=0, tiled=True),
    )
    query_columns = own_head * group_width
    key_columns = own_head * head_size
    pair_queries = lax.dynamic_slice_in_dim(
        lax.dynamic_slice_in_dim(every_query, row_start, draft_rows, 0),
        query_columns,
        group_width,
        1,
    )
    pair_keys = lax.dynamic_slice_in_dim(
        lax.dynamic_slice_in_dim(every_key, row_start, draft_rows, 0), key_columns, head_size, 1
    )
    pair_values = lax.dynamic_slice_in_dim(
        lax.dynamic_slice_in_dim(every_value, row_start, draft_rows, 0), key_columns, head_size, 1
    )
    own_head = jnp.sum(picker * device_head)
    query_rows = pair_queries.reshape(draft_rows, group, head_size)
    own_valid = (
        lax.dynamic_index_in_dim(draft_mask, own_sequence, 0, keepdims=False) > 0
    ) & is_last
    running, total, weighted = attend(
        query_rows, cache_keys, cache_values, own_length, pair_keys, pair_values, own_valid
    )
    block_output = (weighted / total[..., None]).astype(jnp.bfloat16)
    slot_peak = lax.dynamic_update_slice(
        jnp.full((all_rows, group), very_low, jnp.float32), running, (row_start, jnp.int32(0))
    ).reshape(devices, local_rows, group)
    slot_total = lax.dynamic_update_slice(
        jnp.zeros((all_rows, group), jnp.float32), total, (row_start, jnp.int32(0))
    ).reshape(devices, local_rows, group)
    slot_output = lax.dynamic_update_slice(
        jnp.zeros((all_rows, group, head_size), jnp.bfloat16),
        block_output,
        (row_start, jnp.int32(0), jnp.int32(0)),
    ).reshape(devices, local_rows, group, head_size)
    back_peak, back_total = (
        lax.all_to_all(slot_peak, "wide", split_axis=0, concat_axis=0, tiled=True),
        lax.all_to_all(slot_total, "wide", split_axis=0, concat_axis=0, tiled=True),
    )
    back_output = lax.all_to_all(slot_output, "wide", split_axis=0, concat_axis=0, tiled=True)
    member = device_head[:, None] == head_numbers[None, :]
    spread = jnp.where(member[:, None, :, None], back_peak[:, :, None, :], very_low)
    highest = jnp.max(spread, axis=0)
    mixing = jnp.exp(spread - highest[None]) * back_total[:, :, None, :]
    row_total = jnp.sum(mixing, axis=0)
    row_weighted = jnp.einsum(
        "srgj,srjc->rgjc", mixing, back_output.astype(jnp.float32), precision=lax.Precision.HIGHEST
    )
    attended_rows = (
        (row_weighted / row_total[..., None])
        .astype(jnp.bfloat16)
        .reshape(local_rows, heads_all * head_size)
    )
    combined = jnp.dot(
        lax.all_gather(attended_rows, "wide", axis=0, tiled=True),
        out_weight,
        preferred_element_type=jnp.float32,
    )
    projected = combined.astype(jnp.bfloat16)
    columns = projected.shape[1]
    branch = lax.optimization_barrier(projected).astype(jnp.float32)
    squares = lax.psum(jnp.sum(branch * branch, axis=1), "wide")
    inverse = lax.rsqrt(squares / (columns * devices) + epsilon)
    gain_part = lax.dynamic_slice_in_dim(norm_gain, own_index * columns, columns, 0)
    normed = (branch * inverse[:, None] * gain_part[None, :]).astype(jnp.bfloat16)
    piece = lax.all_gather(normed, "wide", axis=1, tiled=True)
    gate = jnp.dot(piece, gate_weight, preferred_element_type=jnp.float32)
    upward = jnp.dot(piece, up_weight, preferred_element_type=jnp.float32)
    hidden = (jax.nn.silu(gate) * upward).astype(jnp.bfloat16)
    return (projected, hidden)


def solution(mesh):
    placed = (
        P(("grp", "wide"), None),
        P(("grp", "wide"), None),
        P(("grp", "wide"), None),
        P(("grp", "wide"), None),
        P(("grp", "wide"), None),
        P("grp"),
        P("grp"),
        P("grp", None, None),
        P(None, "wide"),
        P(),
        P(None, "wide"),
        P(None, "wide"),
    )
    return jax.shard_map(
        per_device,
        mesh=mesh,
        in_specs=placed,
        out_specs=(P("grp", "wide"), P("grp", "wide")),
        check_vma=False,
    )
```

profile of v0, /device:TPU:0, one launch (start us, length us, event | category | flops | bytes accessed | tf_op | source)
XLA Modules:
  0.0 300.9 jit_solution(8862913507777741700)
XLA Ops:
  7.2 0.7 all-gather.4.cloned.1.call-update
  7.9 0.8 select_reduce_fusion.2
  8.7 0.8 select_reduce_fusion.4
  12.1 0.6 select_reduce_fusion.5
  16.7 23.9 %all_gather.16 = bf16[128,512]{1,0:T(8,128)(2,1)S(1)} all-gather(bf16[8,512]{1,0:T(8,128)(2,1)} %param.15), channel_id=1, replica_groups=mesh['grp'=2,'wide'=16] {'wide'}, dimensions={0}, use_global_device_ids=true | all-gather | bytes 139264 | tf_op jit(solution)/shard_map/all_gather | solution.py:98
  40.6 0.8 fusion.41
  41.4 9.5 %all-gather.4.cloned.1.call-done = bf16[128,4096]{1,0:T(8,128)(2,1)} async-done(((bf16[8,4096]{1,0:T(8,128)(2,1)}), bf16[128,4096]{1,0:T(8,128)(2,1)}) %all-gather.4.cloned.1.call-update) | async-done | bytes 1048592 | tf_op jit(solution)/shard_map/all_gather | solution.py:97
  50.9 1.0 dynamic-slice_bitcast_fusion.1
  52.0 0.4 fusion.49
  52.5 11.5 %while.15 = (s32[]{:T(128)}, f32[64,8]{0,1:T(8,128)S(1)}, f32[64,8]{0,1:T(8,128)S(1)}, f32[64,8,128]{2,1,0:T(8,128)S(1)}, s32[]{:T(128)}, /*index=5*/s32[]{:T(12...) while((s32[]{:T(128)}, f32[64,8]{0,1:T(8,128)S(1)}, ...), condition=%wide.region_8.9_spmd.clone, body=%wide.region_5.8_spmd.clone.sunk | while | flops 136185856 | bytes 4099771 | solution.py:51
  52.5 0.7 fusion.68
  53.3 1.3 fusion.69
  54.5 0.4 fusion.70
  55.0 1.3 convolution_add_fusion.3
  56.4 0.7 fusion.68
  57.1 1.3 fusion.69
  58.4 0.4 fusion.70
  58.9 1.3 convolution_add_fusion.3
  60.2 0.7 fusion.68
  60.9 1.3 fusion.69
  62.2 0.4 fusion.70
  62.7 1.3 convolution_add_fusion.3
  64.1 0.2 fusion.25
  64.4 0.3 dynamic_update_slice.11
  64.8 0.7 copy.68
  65.5 52.4 %all-to-all-start.2 = ((f32[16,8,8]{1,2,0:T(8,128)}), f32[16,8,8]{1,2,0:T(8,128)S(1)}, u32[]{:S(2)}, u32[]{:S(2)}) async-start(f32[16,8,8]{1,2,0:T(8,128)} %copy.68), calls=%async_computation.2 | async-start | bytes 131072 | tf_op jit(solution)/shard_map/all_to_all | solution.py:137
  117.9 22.1 %all_gather.17 = bf16[128,512]{1,0:T(8,128)(2,1)S(1)} all-gather(bf16[8,512]{1,0:T(8,128)(2,1)S(1)} %copy-done.2), channel_id=1, replica_groups=mesh['grp'=2,'wide'=16] {'wide'}, dimensions={0}, use_global_device_ids=true | all-gather | bytes 139264 | tf_op jit(solution)/shard_map/all_gather | solution.py:99
  140.0 0.3 dynamic_update_slice.10
  140.5 0.7 copy.66
  141.1 3.5 %all-to-all-start.1 = ((f32[16,8,8]{1,2,0:T(8,128)}), f32[16,8,8]{1,2,0:T(8,128)S(1)}, u32[]{:S(2)}, u32[]{:S(2)}) async-start(f32[16,8,8]{1,2,0:T(8,128)} %copy.66), calls=%async_computation.1 | async-start | bytes 131072 | tf_op jit(solution)/shard_map/all_to_all | solution.py:136
  144.6 0.7 broadcast_in_dim.96
  145.4 0.9 fusion.18
  146.3 5.2 %all-to-all-done.1 = f32[16,8,8]{1,2,0:T(8,128)S(1)} async-done(((f32[16,8,8]{1,2,0:T(8,128)}), f32[16,8,8]{1,2,0:T(8,128)S(1)}, u32[]{:S(2)}, u32[]{:S(2)}) %all-to-all-start.1) | async-done | bytes 4128 | tf_op jit(solution)/shard_map/all_to_all | solution.py:136
  151.5 3.5 %all-to-all-start = ((bf16[16,8,8,128]{3,2,1,0:T(8,128)(2,1)}), bf16[16,8,8,128]{3,2,1,0:T(8,128)(2,1)S(1)}, u32[]{:S(2)}, u32[]{:S(2)}) async-start(bf16[16,8,8,128]{3,2,1,0:T(8,128)(2,1)} %bitcast.3), calls=%async_computation | async-start | bytes 524288 | tf_op jit(solution)/shard_map/all_to_all | solution.py:139
  155.3 0.2 select_reduce_fusion
  155.4 0.3 fusion.29
  155.7 9.3 %all-to-all-done = bf16[16,8,8,128]{3,2,1,0:T(8,128)(2,1)S(1)} async-done(((bf16[16,8,8,128]{3,2,1,0:T(8,128)(2,1)}), bf16[16,8,8,128]{3,2,1,0:T(8,128)(2,1)S(1)}, u32[]{:S(2)}, u32[]{:S(2)}) %all-to-all-start) | async-done | bytes 262176 | tf_op jit(solution)/shard_map/all_to_all | solution.py:139
  165.0 0.5 fusion.20
  165.6 0.7 copy.83
  166.3 0.8 dynamic_slice.29
  167.1 36.5 %all-gather.6.cloned.1.call-done = bf16[128,4096]{1,0:T(8,128)(2,1)} async-done(((bf16[8,4096]{1,0:T(8,128)(2,1)}), bf16[128,4096]{1,0:T(8,128)(2,1)}) %all-gather.6.cloned.1.call-update) | async-done | bytes 1048592 | tf_op jit(solution)/shard_map/all_gather | solution.py:154
  203.5 3.2 %convolution_convert_fusion = bf16[128,512]{1,0:T(8,128)(2,1)S(1)} fusion(bf16[128,4096]{1,0:T(8,128)(2,1)} %all-gather.6.cloned.1.call-done, bf16[4096,512]{1,0:T(8,128)(2,1)} %param.22), kind=kOutput, calls=%fused_computation.27 | convolution fusion | flops 536936448 | bytes 5373952 | tf_op jit(solution)/shard_map/dot_general | solution.py:153
  206.8 0.1 fusion.21
  206.9 31.6 %psum.7 = f32[128]{0:T(128)S(1)} all-reduce(f32[128]{0:T(128)S(1)} %fusion.21), channel_id=1, replica_groups=mesh['grp'=2,'wide'=16] {'wide'}, use_global_device_ids=true, to_apply=%region_15.16 | all-reduce | flops 128 | bytes 1024 | tf_op jit(solution)/shard_map/psum | solution.py:161
  238.5 0.8 fusion.23
  239.3 38.4 %all-gather.8.cloned.1.call-done = bf16[128,8192]{1,0:T(8,128)(2,1)} async-done(((bf16[128,512]{1,0:T(8,128)(2,1)}), bf16[128,8192]{1,0:T(8,128)(2,1)}) %all-gather.8.cloned.1.call-update) | async-done | bytes 2097168 | tf_op jit(solution)/shard_map/all_gather | solution.py:165
  277.7 8.3 %fusion.50 = f32[128,896]{1,0:T(8,128)S(1)} fusion(bf16[128,8192]{1,0:T(8,128)(2,1)} %all-gather.8.cloned.1.call-done, bf16[8192,896]{1,0:T(8,128)(2,1)} %param.24), kind=kOutput, calls=%fused_computation.90 | convolution fusion | flops 1879048192 | bytes 17235968 | tf_op jit(solution)/shard_map/dot_general | solution.py:166
  286.1 8.3 %fusion.14 = bf16[128,896]{1,0:T(8,128)(2,1)} fusion(bf16[128,8192]{1,0:T(8,128)(2,1)S(1)} %copy-done, bf16[8192,896]{1,0:T(8,128)(2,1)} %param.25, f32[128,896]{1,0:T(8,128)S(1)} %fusion.50), kind=kOutput, calls=%fused_computation.20 | convolution fusion | flops 1879736320 | bytes 17465344 | tf_op jit(solution)/shard_map/dot_general | solution.py:167
  (45 shorter events, 1.3 us)
Async XLA Ops:
  7.2 43.8 %all-gather.4.cloned.1.call-start = ((), (), s32[]{:S(2)}) async-start(), calls=%async_computation.3 | async-start | bytes 1114112 | tf_op jit(solution)/shard_map/all_gather | solution.py:97
  52.5 65.3 %copy-start.2 = (bf16[8,512]{1,0:T(8,128)(2,1)S(1)}, bf16[8,512]{1,0:T(8,128)(2,1)}, u32[]{:S(2)}) copy-start(bf16[8,512]{1,0:T(8,128)(2,1)} %param.16) | copy-start | bytes 24580
  65.5 75.7 %all-to-all-start.2 = ((f32[16,8,8]{1,2,0:T(8,128)}), f32[16,8,8]{1,2,0:T(8,128)S(1)}, u32[]{:S(2)}, u32[]{:S(2)}) async-start(f32[16,8,8]{1,2,0:T(8,128)} %copy.68), calls=%async_computation.2 | async-start | bytes 131072 | tf_op jit(solution)/shard_map/all_to_all | solution.py:137
  141.1 10.4 %all-to-all-start.1 = ((f32[16,8,8]{1,2,0:T(8,128)}), f32[16,8,8]{1,2,0:T(8,128)S(1)}, u32[]{:S(2)}, u32[]{:S(2)}) async-start(f32[16,8,8]{1,2,0:T(8,128)} %copy.66), calls=%async_computation.1 | async-start | bytes 131072 | tf_op jit(solution)/shard_map/all_to_all | solution.py:136
  151.5 13.5 %all-to-all-start = ((bf16[16,8,8,128]{3,2,1,0:T(8,128)(2,1)}), bf16[16,8,8,128]{3,2,1,0:T(8,128)(2,1)S(1)}, u32[]{:S(2)}, u32[]{:S(2)}) async-start(bf16[16,8,8,128]{3,2,1,0:T(8,128)(2,1)} %bitcast.3), calls=%async_computation | async-start | bytes 524288 | tf_op jit(solution)/shard_map/all_to_all | solution.py:139
  155.0 48.5 %all-gather.6.cloned.1.call-start = ((), (), s32[]{:S(2)}) async-start(), calls=%async_computation.4 | async-start | bytes 1114112 | tf_op jit(solution)/shard_map/all_gather | solution.py:154
  166.3 111.5 %all-gather.8.cloned.1.call-start = ((), (), s32[]{:S(2)}) async-start(), calls=%async_computation.5 | async-start | bytes 2228224 | tf_op jit(solution)/shard_map/all_gather | solution.py:165
  206.8 79.3 %copy-start.1 = (bf16[128,512]{1,0:T(8,128)(2,1)}, bf16[128,512]{1,0:T(8,128)(2,1)S(1)}, u32[]{:S(2)}) copy-start(bf16[128,512]{1,0:T(8,128)(2,1)S(1)} %convolution_convert_fusion) | copy-start | bytes 393220
  277.7 8.3 %copy-start = (bf16[128,8192]{1,0:T(8,128)(2,1)S(1)}, bf16[128,8192]{1,0:T(8,128)(2,1)}, u32[]{:S(2)}) copy-start(bf16[128,8192]{1,0:T(8,128)(2,1)} %all-gather.8.cloned.1.call-done) | copy-start | bytes 6291460
Sparse Core Ops, SparseCore 0:
  10.1 40.7 all-gather.3
  166.4 37.1 all-gather.5
  239.4 38.2 all-gather.7
where the time goes:
time: 302 us; the launch traced here: 301 us
  waiting for transfers between devices  99.6 us (33%)
  blocking collectives  77.6 us (26%)
  starting transfers between devices  59.5 us (20%)
  matrix products  29.6 us (10%)
  between operations  20.6 us (7%)
  other arithmetic  7.69 us (3%)
  local copies, waits for them, and re-layouts  6.13 us (2%)
    all_to_all x1, starting transfers between devices, per_device(): lax.all_to_all(slot_total, 'wide', split_axis=0, concat_axis=0, tiled=True)  52.4 us
    all_gather x1, waiting for transfers between devices, per_device(): piece = lax.all_gather(normed, 'wide', axis=1, tiled=True)  38.4 us
    all_gather x1, waiting for transfers between devices, per_device(): lax.all_gather(attended_rows, 'wide', axis=0, tiled=True)  36.5 us
    psum x1, blocking collectives, per_device(): squares = lax.psum(jnp.sum(branch * branch, axis=1), 'wide')  31.6 us
    all_gather x1, blocking collectives, per_device(): lax.all_gather(draft_keys, 'wide', axis=0, tiled=True)  23.9 us
    all_gather x1, blocking collectives, per_device(): lax.all_gather(draft_values, 'wide', axis=0, tiled=True)  22.1 us
    all_gather x1, waiting for transfers between devices, per_device(): lax.all_gather(queries, 'wide', axis=0, tiled=True)  9.54 us
    all_to_all x1, waiting for transfers between devices, per_device(): lax.all_to_all(slot_output, 'wide', split_axis=0, concat_axis=0, tiled=True)  9.29 us
  transfers between devices with their start and end apart: 6, of which 5 were waited for; matrix products, arithmetic and copies ran while one was open for 2% of the time, Pallas kernels for 0%

commit v1 on v0

--- a/solution.py
+++ b/solution.py
@@ -158,7 +158,7 @@
     projected = combined.astype(jnp.bfloat16)
     columns = projected.shape[1]
     branch = lax.optimization_barrier(projected).astype(jnp.float32)
-    squares = lax.psum(jnp.sum(branch * branch, axis=1), "wide")
+    squares = jnp.sum(lax.all_gather(jnp.sum(branch * branch, axis=1), "wide"), axis=0)
     inverse = lax.rsqrt(squares / (columns * devices) + epsilon)
     gain_part = lax.dynamic_slice_in_dim(norm_gain, own_index * columns, columns, 0)
     normed = (branch * inverse[:, None] * gain_part[None, :]).astype(jnp.bfloat16)

time: 302 us -> 290 us (0.960)
  blocking collectives: 77.6 us -> 65.4 us
    psum x1 -> x0, blocking collectives: 31.6 us -> none  [per_device(): squares = lax.psum(jnp.sum(branch * branch, axis=1), 'wide')]
    all_gather x0 -> x1, blocking collectives: none -> 19.4 us  [per_device(): lax.all_gather(jnp.sum(branch * branch, axis=1), 'wide')]
where the time goes in v1:
time: 290 us; the launch traced here: 289 us
  waiting for transfers between devices  99.6 us (34%)
  blocking collectives  65.4 us (23%)
  starting transfers between devices  59.5 us (21%)
  matrix products  29.6 us (10%)
  between operations  20.6 us (7%)
  other arithmetic  7.72 us (3%)
  local copies, waits for them, and re-layouts  6.13 us (2%)
    all_to_all x1, starting transfers between devices, per_device(): lax.all_to_all(slot_total, 'wide', split_axis=0, concat_axis=0, tiled=True)  52.4 us
    all_gather x1, waiting for transfers between devices, per_device(): piece = lax.all_gather(normed, 'wide', axis=1, tiled=True)  38.4 us
    all_gather x1, waiting for transfers between devices, per_device(): lax.all_gather(attended_rows, 'wide', axis=0, tiled=True)  36.5 us
    all_gather x1, blocking collectives, per_device(): lax.all_gather(draft_keys, 'wide', axis=0, tiled=True)  23.9 us
    all_gather x1, blocking collectives, per_device(): lax.all_gather(draft_values, 'wide', axis=0, tiled=True)  22.1 us
    all_gather x1, blocking collectives, per_device(): lax.all_gather(jnp.sum(branch * branch, axis=1), 'wide')  19.4 us
    all_gather x1, waiting for transfers between devices, per_device(): lax.all_gather(queries, 'wide', axis=0, tiled=True)  9.54 us
    all_to_all x1, waiting for transfers between devices, per_device(): lax.all_to_all(slot_output, 'wide', split_axis=0, concat_axis=0, tiled=True)  9.29 us
  transfers between devices with their start and end apart: 6, of which 5 were waited for; matrix products, arithmetic and copies ran while one was open for 2% of the time, Pallas kernels for 0%

profile of v1, /device:TPU:0, one launch (start us, length us, event | category | flops | bytes accessed | tf_op | source)
XLA Modules:
  0.0 288.7 jit_solution(1832700702973865646)
XLA Ops:
  7.2 0.7 all-gather.6.cloned.1.call-update
  7.9 0.8 select_reduce_fusion.2
  8.7 0.8 select_reduce_fusion.4
  12.1 0.6 select_reduce_fusion.5
  16.7 23.9 %all_gather.22 = bf16[128,512]{1,0:T(8,128)(2,1)S(1)} all-gather(bf16[8,512]{1,0:T(8,128)(2,1)} %param.15), channel_id=1, replica_groups=mesh['grp'=2,'wide'=16] {'wide'}, dimensions={0}, use_global_device_ids=true | all-gather | bytes 139264 | tf_op jit(solution)/shard_map/all_gather | solution.py:98
  40.6 0.8 fusion.41
  41.4 9.5 %all-gather.6.cloned.1.call-done = bf16[128,4096]{1,0:T(8,128)(2,1)} async-done(((bf16[8,4096]{1,0:T(8,128)(2,1)}), bf16[128,4096]{1,0:T(8,128)(2,1)}) %all-gather.6.cloned.1.call-update) | async-done | bytes 1048592 | tf_op jit(solution)/shard_map/all_gather | solution.py:97
  50.9 1.0 dynamic-slice_bitcast_fusion.1
  52.0 0.4 fusion.49
  52.5 11.5 %while.15 = (s32[]{:T(128)}, f32[64,8]{0,1:T(8,128)S(1)}, f32[64,8]{0,1:T(8,128)S(1)}, f32[64,8,128]{2,1,0:T(8,128)S(1)}, s32[]{:T(128)}, /*index=5*/s32[]{:T(12...) while((s32[]{:T(128)}, f32[64,8]{0,1:T(8,128)S(1)}, ...), condition=%wide.region_8.9_spmd.clone, body=%wide.region_5.8_spmd.clone.sunk | while | flops 136185856 | bytes 4099771 | solution.py:51
  52.5 0.7 fusion.68
  53.3 1.3 fusion.69
  54.5 0.4 fusion.70
  55.0 1.3 convolution_add_fusion.3
  56.4 0.7 fusion.68
  57.1 1.3 fusion.69
  58.4 0.4 fusion.70
  58.9 1.3 convolution_add_fusion.3
  60.2 0.7 fusion.68
  60.9 1.3 fusion.69
  62.2 0.4 fusion.70
  62.7 1.3 convolution_add_fusion.3
  64.1 0.2 fusion.25
  64.4 0.3 dynamic_update_slice.11
  64.8 0.7 copy.68
  65.5 52.4 %all-to-all-start.2 = ((f32[16,8,8]{1,2,0:T(8,128)}), f32[16,8,8]{1,2,0:T(8,128)S(1)}, u32[]{:S(2)}, u32[]{:S(2)}) async-start(f32[16,8,8]{1,2,0:T(8,128)} %copy.68), calls=%async_computation.2 | async-start | bytes 131072 | tf_op jit(solution)/shard_map/all_to_all | solution.py:137
  117.9 22.1 %all_gather.23 = bf16[128,512]{1,0:T(8,128)(2,1)S(1)} all-gather(bf16[8,512]{1,0:T(8,128)(2,1)S(1)} %copy-done.2), channel_id=1, replica_groups=mesh['grp'=2,'wide'=16] {'wide'}, dimensions={0}, use_global_device_ids=true | all-gather | bytes 139264 | tf_op jit(solution)/shard_map/all_gather | solution.py:99
  140.0 0.3 dynamic_update_slice.10
  140.5 0.7 copy.66
  141.1 3.5 %all-to-all-start.1 = ((f32[16,8,8]{1,2,0:T(8,128)}), f32[16,8,8]{1,2,0:T(8,128)S(1)}, u32[]{:S(2)}, u32[]{:S(2)}) async-start(f32[16,8,8]{1,2,0:T(8,128)} %copy.66), calls=%async_computation.1 | async-start | bytes 131072 | tf_op jit(solution)/shard_map/all_to_all | solution.py:136
  144.6 0.7 broadcast_in_dim.96
  145.4 0.9 fusion.18
  146.3 5.2 %all-to-all-done.1 = f32[16,8,8]{1,2,0:T(8,128)S(1)} async-done(((f32[16,8,8]{1,2,0:T(8,128)}), f32[16,8,8]{1,2,0:T(8,128)S(1)}, u32[]{:S(2)}, u32[]{:S(2)}) %all-to-all-start.1) | async-done | bytes 4128 | tf_op jit(solution)/shard_map/all_to_all | solution.py:136
  151.5 3.5 %all-to-all-start = ((bf16[16,8,8,128]{3,2,1,0:T(8,128)(2,1)}), bf16[16,8,8,128]{3,2,1,0:T(8,128)(2,1)S(1)}, u32[]{:S(2)}, u32[]{:S(2)}) async-start(bf16[16,8,8,128]{3,2,1,0:T(8,128)(2,1)} %bitcast.3), calls=%async_computation | async-start | bytes 524288 | tf_op jit(solution)/shard_map/all_to_all | solution.py:139
  155.3 0.2 select_reduce_fusion
  155.4 0.3 fusion.29
  155.7 9.3 %all-to-all-done = bf16[16,8,8,128]{3,2,1,0:T(8,128)(2,1)S(1)} async-done(((bf16[16,8,8,128]{3,2,1,0:T(8,128)(2,1)}), bf16[16,8,8,128]{3,2,1,0:T(8,128)(2,1)S(1)}, u32[]{:S(2)}, u32[]{:S(2)}) %all-to-all-start) | async-done | bytes 262176 | tf_op jit(solution)/shard_map/all_to_all | solution.py:139
  165.0 0.5 fusion.20
  165.6 0.7 copy.83
  166.3 0.8 dynamic_slice.29
  167.1 36.5 %all-gather.8.cloned.1.call-done = bf16[128,4096]{1,0:T(8,128)(2,1)} async-done(((bf16[8,4096]{1,0:T(8,128)(2,1)}), bf16[128,4096]{1,0:T(8,128)(2,1)}) %all-gather.8.cloned.1.call-update) | async-done | bytes 1048592 | tf_op jit(solution)/shard_map/all_gather | solution.py:154
  203.5 3.2 %convolution_convert_fusion = bf16[128,512]{1,0:T(8,128)(2,1)S(1)} fusion(bf16[128,4096]{1,0:T(8,128)(2,1)} %all-gather.8.cloned.1.call-done, bf16[4096,512]{1,0:T(8,128)(2,1)} %param.22), kind=kOutput, calls=%fused_computation.27 | convolution fusion | flops 536936448 | bytes 5373952 | tf_op jit(solution)/shard_map/dot_general | solution.py:153
  206.8 0.1 fusion.21
  206.9 19.4 %all-gather.1 = f32[16,1,128]{2,1,0:T(1,128)S(1)} all-gather(f32[1,1,128]{2,1,0:T(1,128)S(1)} %bitcast.65), channel_id=2, replica_groups=mesh['grp'=2,'wide'=16] {'wide'}, dimensions={0}, use_global_device_ids=true | all-gather | bytes 8704 | tf_op jit(solution)/shard_map/all_gather | solution.py:161
  226.3 0.8 fusion.23
  227.1 38.4 %all-gather.10.cloned.1.call-done = bf16[128,8192]{1,0:T(8,128)(2,1)} async-done(((bf16[128,512]{1,0:T(8,128)(2,1)}), bf16[128,8192]{1,0:T(8,128)(2,1)}) %all-gather.10.cloned.1.call-update) | async-done | bytes 2097168 | tf_op jit(solution)/shard_map/all_gather | solution.py:165
  265.6 8.3 %fusion.50 = f32[128,896]{1,0:T(8,128)S(1)} fusion(bf16[128,8192]{1,0:T(8,128)(2,1)} %all-gather.10.cloned.1.call-done, bf16[8192,896]{1,0:T(8,128)(2,1)} %param.24), kind=kOutput, calls=%fused_computation.90 | convolution fusion | flops 1879048192 | bytes 17235968 | tf_op jit(solution)/shard_map/dot_general | solution.py:166
  273.9 8.3 %fusion.14 = bf16[128,896]{1,0:T(8,128)(2,1)} fusion(bf16[128,8192]{1,0:T(8,128)(2,1)S(1)} %copy-done, bf16[8192,896]{1,0:T(8,128)(2,1)} %param.25, f32[128,896]{1,0:T(8,128)S(1)} %fusion.50), kind=kOutput, calls=%fused_computation.20 | convolution fusion | flops 1879736320 | bytes 17465344 | tf_op jit(solution)/shard_map/dot_general | solution.py:167
  (46 shorter events, 1.4 us)
Async XLA Ops:
  7.2 43.8 %all-gather.6.cloned.1.call-start = ((), (), s32[]{:S(2)}) async-start(), calls=%async_computation.3 | async-start | bytes 1114112 | tf_op jit(solution)/shard_map/all_gather | solution.py:97
  52.5 65.3 %copy-start.2 = (bf16[8,512]{1,0:T(8,128)(2,1)S(1)}, bf16[8,512]{1,0:T(8,128)(2,1)}, u32[]{:S(2)}) copy-start(bf16[8,512]{1,0:T(8,128)(2,1)} %param.16) | copy-start | bytes 24580
  65.5 75.7 %all-to-all-start.2 = ((f32[16,8,8]{1,2,0:T(8,128)}), f32[16,8,8]{1,2,0:T(8,128)S(1)}, u32[]{:S(2)}, u32[]{:S(2)}) async-start(f32[16,8,8]{1,2,0:T(8,128)} %copy.68), calls=%async_computation.2 | async-start | bytes 131072 | tf_op jit(solution)/shard_map/all_to_all | solution.py:137
  141.1 10.4 %all-to-all-start.1 = ((f32[16,8,8]{1,2,0:T(8,128)}), f32[16,8,8]{1,2,0:T(8,128)S(1)}, u32[]{:S(2)}, u32[]{:S(2)}) async-start(f32[16,8,8]{1,2,0:T(8,128)} %copy.66), calls=%async_computation.1 | async-start | bytes 131072 | tf_op jit(solution)/shard_map/all_to_all | solution.py:136
  151.5 13.5 %all-to-all-start = ((bf16[16,8,8,128]{3,2,1,0:T(8,128)(2,1)}), bf16[16,8,8,128]{3,2,1,0:T(8,128)(2,1)S(1)}, u32[]{:S(2)}, u32[]{:S(2)}) async-start(bf16[16,8,8,128]{3,2,1,0:T(8,128)(2,1)} %bitcast.3), calls=%async_computation | async-start | bytes 524288 | tf_op jit(solution)/shard_map/all_to_all | solution.py:139
  155.0 48.5 %all-gather.8.cloned.1.call-start = ((), (), s32[]{:S(2)}) async-start(), calls=%async_computation.4 | async-start | bytes 1114112 | tf_op jit(solution)/shard_map/all_gather | solution.py:154
  166.3 99.3 %all-gather.10.cloned.1.call-start = ((), (), s32[]{:S(2)}) async-start(), calls=%async_computation.5 | async-start | bytes 2228224 | tf_op jit(solution)/shard_map/all_gather | solution.py:165
  206.8 67.1 %copy-start.1 = (bf16[128,512]{1,0:T(8,128)(2,1)}, bf16[128,512]{1,0:T(8,128)(2,1)S(1)}, u32[]{:S(2)}) copy-start(bf16[128,512]{1,0:T(8,128)(2,1)S(1)} %convolution_convert_fusion) | copy-start | bytes 393220
  265.6 8.3 %copy-start = (bf16[128,8192]{1,0:T(8,128)(2,1)S(1)}, bf16[128,8192]{1,0:T(8,128)(2,1)}, u32[]{:S(2)}) copy-start(bf16[128,8192]{1,0:T(8,128)(2,1)} %all-gather.10.cloned.1.call-done) | copy-start | bytes 6291460
Sparse Core Ops, SparseCore 0:
  10.1 40.7 all-gather.5
  166.4 37.1 all-gather.7
  227.3 38.2 all-gather.9
